TPU v7x, 32 devices: a whole 2x2x4 slice. The times are simulated.
32 devices in a mesh: replica: 4 (over y, x), shard: 8 (over z, core).
Axes of the slice: x: 2, y: 2, z: 4, core: 2. Of those that a mesh axis runs over, the one named last changes fastest.
Arguments:
- block_input: float32 [32, 224, 768], P(('replica', 'shard')), may hold values from -6 to 6
- out_cotangent: float32 [32, 224, 768], P(('replica', 'shard')), may hold values from -6 to 6
- ln1_gain: bfloat16 [768], P('shard'), may hold values from 0.5 to 1.5
- ln1_bias: bfloat16 [768], P('shard'), may hold values from -3 to 3
- attn_query: bfloat16 [768, 768], P('shard'), as said below
- query_bias: bfloat16 [768], P('shard'), may hold values from -3 to 3
- attn_key: bfloat16 [768, 768], P('shard'), may hold values from -0.21875 to 0.21875
- attn_value: bfloat16 [768, 768], P('shard'), may hold values from -0.21875 to 0.21875
- value_bias: bfloat16 [768], P('shard'), may hold values from -3 to 3
- attn_out: bfloat16 [768, 768], P('shard'), may hold values from -2 to 2
- out_bias: bfloat16 [768], P('shard'), may hold values from -3 to 3
- ln2_gain: bfloat16 [768], P('shard'), may hold values from 0.5 to 1.5
- ln2_bias: bfloat16 [768], P('shard'), may hold values from -3 to 3
- fc1_weight: bfloat16 [768, 3072], P('shard'), may hold values from -0.21875 to 0.21875
- fc1_bias: bfloat16 [3072], P('shard'), may hold values from -3 to 3
- fc2_weight: bfloat16 [3072, 768], P('shard'), may hold values from -0.21875 to 0.21875
- fc2_bias: bfloat16 [768], P('shard'), may hold values from -3 to 3
Outputs:
- block_output: float32 [32, 224, 768], P(('replica', 'shard'))
- input_grad: float32 [32, 224, 768], P(('replica', 'shard'))
- ln1_gain_grad: float32 [768], P('shard')
- ln1_bias_grad: float32 [768], P('shard')
- query_grad: float32 [768, 768], P('shard')
- query_bias_grad: float32 [768], P('shard')
- key_grad: float32 [768, 768], P('shard')
- value_grad: float32 [768, 768], P('shard')
- value_bias_grad: float32 [768], P('shard')
- out_grad: float32 [768, 768], P('shard')
- out_bias_grad: float32 [768], P('shard')
- ln2_gain_grad: float32 [768], P('shard')
- ln2_bias_grad: float32 [768], P('shard')
- fc1_grad: float32 [768, 3072], P('shard')
- fc1_bias_grad: float32 [3072], P('shard')
- fc2_grad: float32 [3072, 768], P('shard')
- fc2_bias_grad: float32 [768], P('shard')
Inputs may be any that keep to these rules, and one draw needn't show every extreme that they name: `attn_query`: weights of the query projection.
All inputs are finite; a program needn't handle non-finite values.
Results may differ from a plain program's by a relative error of at most 0.014.
The roundings to bfloat16 on the way count: a program that leaves them out, or rounds other values in their place, can miss the bound.
Values may be sent and summed in bfloat16 or wider, within the bound.
A program may use at most 128 MiB of HBM per device.

v0:
```python
import jax
import jax.numpy as jnp
from jax import lax
from jax.sharding import PartitionSpec as P

HEADS = 12
HEAD_DIM = 64


def matmul(spec, left, right):
    return jnp.einsum(spec, left, right, preferred_element_type=jnp.float32)


def normalize(inputs, gain, shift):
    center = inputs - jnp.mean(inputs, axis=-1, keepdims=True)
    inv_std = lax.rsqrt(jnp.mean(center * center, axis=-1, keepdims=True) + 1e-05)
    normed = center * inv_std
    act = (normed * gain.astype(jnp.float32) + shift.astype(jnp.float32)).astype(jnp.bfloat16)
    return (normed, inv_std, act)


def norm_back(grad_out, normed, inv_std, gain):
    scaled = grad_out * gain.astype(jnp.float32)
    return inv_std * (
        scaled
        - jnp.mean(scaled, axis=-1, keepdims=True)
        - normed * jnp.mean(scaled * normed, axis=-1, keepdims=True)
    )


def gelu_parts(pre):
    cdf = 0.5 * (1.0 + jax.scipy.special.erf(pre * 0.7071067811865476))
    dens = jnp.exp(-0.5 * pre * pre) * 0.3989422804014327
    return (pre * cdf, cdf + pre * dens)


def forward_pass(block_input, attn_full, mlp_full):
    ln1_gain, ln1_bias, attn_qkv, query_bias, value_bias, attn_out, out_bias = attn_full
    ln2_gain, ln2_bias, fc1_weight, fc1_bias, fc2_weight, fc2_bias = mlp_full
    f32 = jnp.float32
    bf16 = jnp.bfloat16
    clips, frames, width = block_input.shape
    scale = HEAD_DIM ** (-0.5)
    heads_shape = (clips, frames, HEADS, HEAD_DIM)
    normed1, inv1, act1 = normalize(block_input, ln1_gain, ln1_bias)
    mixed_in = matmul("cld,de->cle", act1, attn_qkv)
    query = ((mixed_in[..., :width] + query_bias.astype(f32)) * scale).astype(bf16)
    keys = mixed_in[..., width : 2 * width].astype(bf16)
    values = (mixed_in[..., 2 * width :] + value_bias.astype(f32)).astype(bf16)
    query, keys, values = (part.reshape(heads_shape) for part in (query, keys, values))
    scores = matmul("clhe,cmhe->chlm", query, keys)
    top = jnp.max(scores, axis=-1, keepdims=True)
    log_total = top + jnp.log(jnp.sum(jnp.exp(scores - top), axis=-1, keepdims=True))
    probs = jnp.exp(scores - log_total)
    mixed = (
        matmul("chlm,cmhe->clhe", probs.astype(bf16), values)
        .astype(bf16)
        .reshape(clips, frames, width)
    )
    middle = block_input + matmul("cld,de->cle", mixed, attn_out) + out_bias.astype(f32)
    normed2, inv2, act2 = normalize(middle, ln2_gain, ln2_bias)
    pre = matmul("cld,df->clf", act2, fc1_weight) + fc1_bias.astype(f32)
    activ, slope = gelu_parts(pre)
    activ_b = activ.astype(bf16)
    block_output = middle + matmul("clf,fd->cld", activ_b, fc2_weight) + fc2_bias.astype(f32)
    saved = (
        normed1,
        inv1,
        act1,
        query,
        keys,
        values,
        log_total,
        mixed,
        normed2,
        inv2,
        act2,
        slope,
        activ_b,
    )
    return (block_output, saved)


def backward_pass(out_cotangent, saved, attn_full, mlp_full):
    ln1_gain, ln1_bias, attn_qkv, query_bias, value_bias, attn_out, out_bias = attn_full
    ln2_gain, ln2_bias, fc1_weight, fc1_bias, fc2_weight, fc2_bias = mlp_full
    (
        normed1,
        inv1,
        act1,
        query,
        keys,
        values,
        log_total,
        mixed,
        normed2,
        inv2,
        act2,
        slope,
        activ_b,
    ) = saved
    bf16 = jnp.bfloat16
    clips, frames, width = out_cotangent.shape
    scale = HEAD_DIM ** (-0.5)
    heads_shape = (clips, frames, HEADS, HEAD_DIM)
    grad_b = out_cotangent.astype(bf16)
    fc2_grad = matmul("clf,cld->fd", activ_b, grad_b)
    fc2_bias_grad = jnp.sum(out_cotangent, axis=(0, 1))
    grad_pre = matmul("cld,fd->clf", grad_b, fc2_weight) * slope
    grad_pre_b = grad_pre.astype(bf16)
    fc1_grad = matmul("cld,clf->df", act2, grad_pre_b)
    fc1_bias_grad = jnp.sum(grad_pre, axis=(0, 1))
    grad_act2 = matmul("clf,df->cld", grad_pre_b, fc1_weight)
    ln2_gain_grad = jnp.sum(grad_act2 * normed2, axis=(0, 1))
    ln2_bias_grad = jnp.sum(grad_act2, axis=(0, 1))
    grad_middle = out_cotangent + norm_back(grad_act2, normed2, inv2, ln2_gain)
    grad_mid_b = grad_middle.astype(bf16)
    out_grad = matmul("cld,cle->de", mixed, grad_mid_b)
    out_bias_grad = jnp.sum(grad_middle, axis=(0, 1))
    grad_mixed = matmul("cle,de->cld", grad_mid_b, attn_out).astype(bf16).reshape(heads_shape)
    again = jnp.exp(matmul("clhe,cmhe->chlm", query, keys) - log_total)
    grad_probs = matmul("clhe,cmhe->chlm", grad_mixed, values)
    inner = jnp.sum(again * grad_probs, axis=-1, keepdims=True)
    grad_scores = (again * (grad_probs - inner)).astype(bf16)
    grad_query = matmul("chlm,cmhe->clhe", grad_scores, keys).reshape(clips, frames, width) * scale
    grad_keys = matmul("chlm,clhe->cmhe", grad_scores, query).reshape(clips, frames, width)
    grad_values = matmul("chlm,clhe->cmhe", again.astype(bf16), grad_mixed).reshape(
        clips, frames, width
    )
    query_bias_grad = jnp.sum(grad_query, axis=(0, 1))
    value_bias_grad = jnp.sum(grad_values, axis=(0, 1))
    grad_query_b = grad_query.astype(bf16)
    grad_keys_b = grad_keys.astype(bf16)
    grad_values_b = grad_values.astype(bf16)
    joined = jnp.concatenate((grad_query_b, grad_keys_b, grad_values_b), axis=-1)
    qkv_grad = matmul("cld,cle->de", act1, joined)
    grad_act1 = matmul("cle,de->cld", joined, attn_qkv)
    ln1_gain_grad = jnp.sum(grad_act1 * normed1, axis=(0, 1))
    ln1_bias_grad = jnp.sum(grad_act1, axis=(0, 1))
    input_grad = grad_middle + norm_back(grad_act1, normed1, inv1, ln1_gain)
    attn_grads = (
        ln1_gain_grad,
        ln1_bias_grad,
        qkv_grad,
        query_bias_grad,
        value_bias_grad,
        out_grad,
        out_bias_grad,
    )
    mlp_grads = (ln2_gain_grad, ln2_bias_grad, fc1_grad, fc1_bias_grad, fc2_grad, fc2_bias_grad)
    return (input_grad, attn_grads, mlp_grads)


def body(
    block_input,
    out_cotangent,
    ln1_gain,
    ln1_bias,
    attn_query,
    query_bias,
    attn_key,
    attn_value,
    value_bias,
    attn_out,
    out_bias,
    ln2_gain,
    ln2_bias,
    fc1_weight,
    fc1_bias,
    fc2_weight,
    fc2_bias,
):
    f32 = jnp.float32
    bf16 = jnp.bfloat16
    rows, width = attn_query.shape
    per_row = fc1_bias.shape[0] // rows
    narrow = (ln1_gain, ln1_bias, query_bias, value_bias, out_bias, ln2_gain, ln2_bias, fc2_bias)
    columns = jnp.concatenate((jnp.stack(narrow, axis=1), fc1_bias.reshape(rows, per_row)), axis=1)
    used = columns.shape[1]
    spare = -used % 128
    packed = jnp.concatenate(
        (attn_query, attn_key, attn_value, attn_out, jnp.pad(columns, ((0, 0), (0, spare)))), axis=1
    )
    attn_all = lax.all_gather(packed, "shard", axis=0, tiled=True)
    fc1_all = lax.all_gather(fc1_weight, "shard", axis=0, tiled=True)
    fc2_all = lax.all_gather(fc2_weight, "shard", axis=0, tiled=True)
    small = attn_all[:, 4 * width : 4 * width + used]
    g1, b1, bq, bv, bo, g2, b2, bf2 = (small[:, i] for i in range(len(narrow)))
    bf1 = small[:, len(narrow) :].reshape(-1)
    attn_full = (g1, b1, attn_all[:, : 3 * width], bq, bv, attn_all[:, 3 * width : 4 * width], bo)
    mlp_full = (g2, b2, fc1_all, bf1, fc2_all, bf2)
    block_output, saved = forward_pass(block_input, attn_full, mlp_full)
    input_grad, attn_grads, mlp_grads = backward_pass(out_cotangent, saved, attn_full, mlp_full)
    dg1, db1, dqkv, dbq, dbv, dout, dbo = attn_grads
    dg2, db2, dfc1, dbf1, dfc2, dbf2 = mlp_grads

    def owned(grad):
        part = lax.psum_scatter(grad.astype(bf16), "shard", scatter_dimension=0, tiled=True)
        return lax.psum(part, "replica").astype(f32)

    fc2_owned = owned(dfc2)
    fc1_owned = owned(dfc1)
    thin = jnp.concatenate(
        (jnp.stack((dg1, db1, dbq, dbv, dbo, dg2, db2, dbf2), axis=1), dbf1.reshape(-1, per_row)),
        axis=1,
    )
    attn_owned = owned(jnp.concatenate((dqkv, dout, jnp.pad(thin, ((0, 0), (0, spare)))), axis=1))
    base = 4 * width
    og1, ob1, obq, obv, obo, og2, ob2, obf2 = (attn_owned[:, base + i] for i in range(len(narrow)))
    obf1 = attn_owned[:, base + len(narrow) : base + used].reshape(-1)
    return (
        block_output,
        input_grad,
        og1,
        ob1,
        attn_owned[:, :width],
        obq,
        attn_owned[:, width : 2 * width],
        attn_owned[:, 2 * width : 3 * width],
        obv,
        attn_owned[:, 3 * width : 4 * width],
        obo,
        og2,
        ob2,
        fc1_owned,
        obf1,
        fc2_owned,
        obf2,
    )


def solution(mesh):
    placed = (
        P(("replica", "shard"), None, None),
        P(("replica", "shard"), None, None),
        P("shard"),
        P("shard"),
        P("shard", None),
        P("shard"),
        P("shard", None),
        P("shard", None),
        P("shard"),
        P("shard", None),
        P("shard"),
        P("shard"),
        P("shard"),
        P("shard", None),
        P("shard"),
        P("shard", None),
        P("shard"),
    )
    return jax.shard_map(
        body,
        mesh=mesh,
        in_specs=placed,
        out_specs=(
            P(("replica", "shard"), None, None),
            P(("replica", "shard"), None, None),
            P("shard"),
            P("shard"),
            P("shard", None),
            P("shard"),
            P("shard", None),
            P("shard", None),
            P("shard"),
            P("shard", None),
            P("shard"),
            P("shard"),
            P("shard"),
            P("shard", None),
            P("shard"),
            P("shard", None),
            P("shard"),
        ),
        check_vma=False,
    )
```

profile of v0, /device:TPU:0, one launch (start us, length us, event | category | flops | bytes accessed | tf_op | source)
XLA Modules:
  0.0 430.5 jit_solution(5986682349822183564)
XLA Ops:
  7.2 0.9 reshape.409
  9.1 0.9 constant_dynamic-update-slice_fusion.3
  10.1 0.9 constant_dynamic-update-slice_fusion.2
  11.0 0.9 constant_dynamic-update-slice_fusion.1
  11.9 0.9 constant_dynamic-update-slice_fusion
  15.6 54.1 %all-gather.4.cloned.1.call-done = bf16[768,3200]{1,0:T(8,128)(2,1)} async-done(((bf16[96,3200]{1,0:T(8,128)(2,1)}), bf16[768,3200]{1,0:T(8,128)(2,1)}) %all-gather.4.cloned.1.call-update) | async-done | bytes 4915216 | tf_op jit(solution)/shard_map/all_gather | solution.py:184
  69.7 1.0 slice_convert_fusion.1
  71.0 3.1 convert_reduce_fusion
  74.1 3.0 convolution_bitcast_fusion
  77.3 0.9 copy.96
  78.2 0.9 copy.97
  79.3 1.8 fusion.55
  82.3 1.9 fusion.56
  84.4 36.8 %all-gather.6.cloned.1.call-done = bf16[768,3072]{1,0:T(8,128)(2,1)} async-done(((bf16[96,3072]{1,0:T(8,128)(2,1)}), bf16[768,3072]{1,0:T(8,128)(2,1)}) %all-gather.6.cloned.1.call-update) | async-done | bytes 4718608 | tf_op jit(solution)/shard_map/all_gather | solution.py:185
  121.2 5.9 %multiply_convert_fusion.1 = (bf16[224,3072]{1,0:T(8,128)(2,1)}, f32[224,3072]{1,0:T(8,128)}) fusion(f32[3072]{0:T(1024)S(1)} %reshape.429, bf16[768,3072]{1,0:T(8,128)(2,1)} %all-gather.6.cloned.1.call-done, f32[1,224,768]{2,1,0:T(8,128)S(1)} %get-tuple-element.60, f32[768]{0:T(1024)S(1)} %get-tuple-element.18, f32[768]{0:T(1024)S(1)} %get-tuple-element.19, ...), kind=kOutput, calls=%fused_computation.19 | convolution fusion | flops 1061953536 | bytes 9555712 | tf_op jit(solution)/shard_map/cld,df->clf/dot_general | solution.py:11
  127.2 45.7 %all-gather.8.cloned.1.call-done = bf16[3072,768]{1,0:T(8,128)(2,1)} async-done(((bf16[384,768]{1,0:T(8,128)(2,1)}), bf16[3072,768]{1,0:T(8,128)(2,1)}) %all-gather.8.cloned.1.call-update) | async-done | bytes 4718608 | tf_op jit(solution)/shard_map/all_gather | solution.py:186
  172.9 5.2 %fusion.57 = (bf16[3072]{0:T(1024)(128)(2,1)S(1)}, bf16[224,3072]{1,0:T(8,128)(2,1)S(1)}) fusion(f32[224,3072]{1,0:T(8,128)} %get-tuple-element.62, bf16[3072,768]{1,0:T(8,128)(2,1)} %all-gather.8.cloned.1.call-done, f32[1,224,768]{2,1,0:T(8,128)} %param.18), kind=kOutput, calls=%fused_computation.121 | convolution fusion | flops 1064702976 | bytes 9541632 | tf_op jit(solution)/shard_map/cld,fd->clf/dot_general | solution.py:11
  178.2 1.2 copy-done.14
  179.3 3.8 convolution_convert_fusion.2
  183.2 5.1 %convolution_convert_fusion.1 = bf16[3072,768]{1,0:T(8,128)(2,1)} fusion(bf16[224,3072]{1,0:T(8,128)(2,1)} %get-tuple-element.61, f32[1,224,768]{2,1,0:T(8,128)} %param.18), kind=kOutput, calls=%fused_computation.3 | convolution fusion | flops 1059495936 | bytes 6782976 | tf_op jit(solution)/shard_map/clf,cld->fd/dot_general | solution.py:11
  188.5 1.1 reshape.420
  189.6 4.5 %fusion.19 = (bf16[768]{0:T(1024)(128)(2,1)S(1)}, f32[224]{0:T(256)S(1)}, f32[224,768]{1,0:T(8,128)S(1)}) fusion(f32[1,224,768]{2,1,0:T(8,128)S(1)} %get-tuple-element.60, f32[224]{0:T(256)S(1)} %add_rsqrt_fusion, f32[224]{0:T(256)S(1)} %broadcast_multiply_fusion.4, f32[768]{0:T(1024)S(1)} %get-tuple-element.19, ...), kind=kOutput, calls=%fused_computation.46 | convolution fusion | flops 1058167808 | bytes 7478400 | tf_op jit(solution)/shard_map/clf,df->cld/dot_general | solution.py:11
  194.7 0.9 stack.76
  195.5 0.9 stack.78
  196.4 0.9 stack.77
  198.1 2.6 convolution_convert_fusion.6
  200.7 1.9 copy.99
  202.6 2.4 fusion.52
  204.9 1.1 stack.75
  206.0 1.9 multiply_reduce_fusion
  208.5 1.1 copy-done
  210.0 1.1 stack.74
  211.1 2.0 convolution_convert_fusion.4
  213.2 3.7 fusion.20
  219.7 2.3 concatenate.20
  222.5 2.6 convolution_convert_fusion
  225.1 2.6 fusion.1
  227.8 9.1 %reduce-scatter.6.cloned.1.call-done = bf16[96,3072]{1,0:T(8,128)(2,1)} async-done(((bf16[768,3072]{1,0:T(8,128)(2,1)}), bf16[96,3072]{1,0:T(8,128)(2,1)}) %reduce-scatter.6.cloned.1.call-update) | async-done | bytes 589840 | tf_op jit(solution)/shard_map/reduce_scatter | solution.py:198
  236.9 55.5 %reduce-scatter.8.cloned.1.call-done = bf16[384,768]{1,0:T(8,128)(2,1)} async-done(((bf16[3072,768]{1,0:T(8,128)(2,1)}), bf16[384,768]{1,0:T(8,128)(2,1)}) %reduce-scatter.8.cloned.1.call-update) | async-done | bytes 589840 | tf_op jit(solution)/shard_map/reduce_scatter | solution.py:198
  292.5 57.4 %reduce-scatter.4.cloned.1.call-done = bf16[96,3200]{1,0:T(8,128)(2,1)} async-done(((bf16[768,3200]{1,0:T(8,128)(2,1)}), bf16[96,3200]{1,0:T(8,128)(2,1)}) %reduce-scatter.4.cloned.1.call-update) | async-done | bytes 614416 | tf_op jit(solution)/shard_map/reduce_scatter | solution.py:198
  349.9 2.2 fusion.23
  352.1 4.4 %fusion.13 = f32[1,224,768]{2,1,0:T(8,128)} fusion(f32[1,224,768]{2,1,0:T(8,128)S(1)} %get-tuple-element.60, bf16[224,3072]{1,0:T(8,128)(2,1)S(1)} %copy-done.11, bf16[3072,768]{1,0:T(8,128)(2,1)} %all-gather.8.cloned.1.call-done, f32[768]{0:T(1024)S(1)} %get-tuple-element.17), kind=kOutput, calls=%fused_computation.34 | convolution fusion | flops 1057308672 | bytes 7474176 | tf_op jit(solution)/shard_map/clf,fd->cld/dot_general | solution.py:11
  356.5 60.1 %all-reduce.5.cloned.1.call-done = (bf16[96,3200]{1,0:T(8,128)(2,1)}, bf16[96,3072]{1,0:T(8,128)(2,1)}, bf16[384,768]{1,0:T(8,128)(2,1)}) async-done(((bf16[96,3200]{1,0:T(8,128)(2,1)}, bf16[96,3072]{1,0:T(8,128)(2,1)}, bf16[384,768]{1,0:T(8,128)(2,1)}), (bf16[96,3200]{1,0:T(8,128)(2,1)}, bf16[96,3072]{1,0:T(8,128)(2,1)}, bf16[384,768]{1,0:T(8,128)(2,1)})) %all-reduce.5.cloned.1.call-update) | async-done | bytes 1794064 | tf_op jit(solution)/shard_map/psum | solution.py:199
  416.7 0.9 slice.144
  417.6 2.2 fusion.54
  420.6 1.1 convert_element_type.259
  421.7 1.1 convert_element_type.261
  422.8 0.9 slice_reduce_fusion
  (98 shorter events, 12.3 us)
Async XLA Ops:
  7.2 8.1 %copy-start.1 = (f32[1,224,768]{2,1,0:T(8,128)S(1)}, f32[1,224,768]{2,1,0:T(8,128)}, u32[]{:S(2)}) copy-start(f32[1,224,768]{2,1,0:T(8,128)} %param.17) | copy-start | bytes 2064388
  7.2 62.5 %all-gather.4.cloned.1.call-start = ((), (), s32[]{:S(2)}) async-start(), calls=%async_computation.3 | async-start | bytes 5529600 | tf_op jit(solution)/shard_map/all_gather | solution.py:184
  12.9 0.8 copy-start.15
  13.7 107.5 %all-gather.6.cloned.1.call-start = ((), (), s32[]{:S(2)}) async-start(), calls=%async_computation.4 | async-start | bytes 5308416 | tf_op jit(solution)/shard_map/all_gather | solution.py:185
  14.5 158.4 %all-gather.8.cloned.1.call-start = ((), (), s32[]{:S(2)}) async-start(), calls=%async_computation.5 | async-start | bytes 5308416 | tf_op jit(solution)/shard_map/all_gather | solution.py:186
  15.2 221.7 %reduce-scatter.6.cloned.1.call-start = ((), (), s32[]{:S(2)}) async-start(), calls=%async_computation.7 | async-start | bytes 5308416 | tf_op jit(solution)/shard_map/reduce_scatter | solution.py:198
  79.3 2.3 copy-start.7
  81.2 1.1 copy-start.2
  82.2 2.0 copy-start.9
  178.1 1.2 copy-start.14
  183.1 109.3 %reduce-scatter.8.cloned.1.call-start = ((), (), s32[]{:S(2)}) async-start(), calls=%async_computation.8 | async-start | bytes 5308416 | tf_op jit(solution)/shard_map/reduce_scatter | solution.py:198
  188.3 161.6 %reduce-scatter.4.cloned.1.call-start = ((), (), s32[]{:S(2)}) async-start(), calls=%async_computation.6 | async-start | bytes 5529600 | tf_op jit(solution)/shard_map/reduce_scatter | solution.py:198
  189.6 4.7 %copy-start.13 = (f32[1,224,768]{2,1,0:T(8,128)S(1)}, f32[1,224,768]{2,1,0:T(8,128)}, u32[]{:S(2)}) copy-start(f32[1,224,768]{2,1,0:T(8,128)} %param.18) | copy-start | bytes 2064388
  194.6 3.5 copy-start.4
  207.9 1.7 copy-start.8
  208.5 1.1 copy-start
  209.6 3.6 copy-start.3
  209.6 3.6 copy-start.24
  210.0 3.1 copy-start.25
  213.2 3.8 copy-start.26
  213.2 6.5 %copy-start.16 = (bf16[768,4]{1,0:T(8,128)(2,1)S(1)}, bf16[768,4]{1,0:T(8,128)(2,1)}, u32[]{:S(2)}) copy-start(bf16[768,4]{1,0:T(8,128)(2,1)} %reshape.420) | copy-start | bytes 18436
  213.2 6.5 %copy-start.17 = (bf16[768,1]{1,0:T(8,128)(2,1)S(1)}, bf16[768,1]{1,0:T(8,128)(2,1)}, u32[]{:S(2)}) copy-start(bf16[768,1]{1,0:T(8,128)(2,1)} %stack.76) | copy-start | bytes 4612
  213.2 6.4 %copy-start.18 = (bf16[768,1]{1,0:T(8,128)(2,1)S(1)}, bf16[768,1]{1,0:T(8,128)(2,1)}, u32[]{:S(2)}) copy-start(bf16[768,1]{1,0:T(8,128)(2,1)} %stack.78) | copy-start | bytes 4612
  213.2 6.4 %copy-start.19 = (bf16[768,1]{1,0:T(8,128)(2,1)S(1)}, bf16[768,1]{1,0:T(8,128)(2,1)}, u32[]{:S(2)}) copy-start(bf16[768,1]{1,0:T(8,128)(2,1)} %stack.77) | copy-start | bytes 4612
  213.2 6.4 %copy-start.20 = (bf16[768,1]{1,0:T(8,128)(2,1)S(1)}, bf16[768,1]{1,0:T(8,128)(2,1)}, u32[]{:S(2)}) copy-start(bf16[768,1]{1,0:T(8,128)(2,1)} %stack.79) | copy-start | bytes 4612
  217.0 0.8 copy-start.12
  217.0 5.0 %copy-start.5 = (f32[1,224,768]{2,1,0:T(8,128)S(1)}, f32[1,224,768]{2,1,0:T(8,128)}, u32[]{:S(2)}) copy-start(f32[1,224,768]{2,1,0:T(8,128)} %copy-done.4) | copy-start | bytes 2064388
  217.0 5.0 %copy-start.10 = (bf16[12,64,224]{2,1,0:T(8,128)(2,1)S(1)}, bf16[12,64,224]{2,1,0:T(8,128)(2,1)}, u32[]{:S(2)}) copy-start(bf16[12,64,224]{2,1,0:T(8,128)(2,1)} %copy-done.9) | copy-start | bytes 1032196
  222.5 2.6 copy-start.21
  227.7 124.4 %copy-start.11 = (bf16[224,3072]{1,0:T(8,128)(2,1)S(1)}, bf16[224,3072]{1,0:T(8,128)(2,1)}, u32[]{:S(2)}) copy-start(bf16[224,3072]{1,0:T(8,128)(2,1)} %get-tuple-element.61) | copy-start | bytes 4128772
  227.7 188.9 %all-reduce.5.cloned.1.call-start = ((), (), s32[]{:S(2)}) async-start(), calls=%async_computation.9 | async-start | bytes 3588096 | tf_op jit(solution)/shard_map/psum | solution.py:199
  416.7 3.1 copy-start.6
  416.7 3.9 copy-start.23
  417.6 4.1 copy-start.22
Sparse Core Ops, SparseCore 0:
  13.8 55.8 all-gather.3
  71.4 49.8 all-gather.5
  122.9 49.9 all-gather.7
  183.3 53.6 reduce-scatter.5
  239.1 53.3 reduce-scatter.7
  294.6 55.1 reduce-scatter.3
  353.4 63.2 all-reduce.4
where the time goes:
time: 431 us; the launch traced here: 430 us
  waiting for transfers between devices  320 us (74%)
  matrix products  52.4 us (12%)
  local copies, waits for them, and re-layouts  29.2 us (7%)
  between operations  14.6 us (3%)
  other arithmetic  13.6 us (3%)
    reduce_scatter x3, waiting for transfers between devices, owned(): lax.psum_scatter(grad.astype(bf16), 'shard', scatter_dimension=0, tiled=T...  122 us
    psum x1, waiting for transfers between devices, owned(): return lax.psum(part, 'replica').astype(f32)  60.1 us
    all_gather x1, waiting for transfers between devices, body(): attn_all = lax.all_gather(packed, 'shard', axis=0, tiled=True)  54.1 us
    dot_general x18, matrix products, matmul(): return jnp.einsum(spec, left, right, preferred_element_type=jnp.float32)  52.4 us
    all_gather x1, waiting for transfers between devices, body(): fc2_all = lax.all_gather(fc2_weight, 'shard', axis=0, tiled=True)  45.7 us
    all_gather x1, waiting for transfers between devices, body(): fc1_all = lax.all_gather(fc1_weight, 'shard', axis=0, tiled=True)  36.8 us
  transfers between devices with their start and end apart: 7, of which 7 were waited for; matrix products, arithmetic and copies ran while one was open for 16% of the time, Pallas kernels for 0%

commit v1 on v0

--- a/solution.py
+++ b/solution.py
@@ -5,6 +5,28 @@
 
 HEADS = 12
 HEAD_DIM = 64
+
+
+def joined_along(blocks, dim):
+    shape = list(blocks.shape[1:])
+    shape[dim] *= blocks.shape[0]
+    return jnp.moveaxis(blocks, 0, dim).reshape(shape)
+
+
+def grow_blocks(x, axis):
+    size = lax.axis_size(axis)
+    pieces = x[None]
+    for level in range(size.bit_length() - 1):
+        stride = 1 << level
+        partner_block = lax.ppermute(pieces, axis, [(i, i ^ stride) for i in range(size)])
+        both = jnp.stack([pieces, partner_block])
+        upper = lax.axis_index(axis) >> level & 1
+        pieces = jnp.where(upper == 0, both, both[::-1]).reshape(-1, *x.shape)
+    return pieces
+
+
+def gather_by_bits(value, axis, dim):
+    return joined_along(grow_blocks(value, axis), dim)
 
 
 def matmul(spec, left, right):
@@ -182,7 +204,7 @@
         (attn_query, attn_key, attn_value, attn_out, jnp.pad(columns, ((0, 0), (0, spare)))), axis=1
     )
     attn_all = lax.all_gather(packed, "shard", axis=0, tiled=True)
-    fc1_all = lax.all_gather(fc1_weight, "shard", axis=0, tiled=True)
+    fc1_all = gather_by_bits(fc1_weight, "shard", 0)
     fc2_all = lax.all_gather(fc2_weight, "shard", axis=0, tiled=True)
     small = attn_all[:, 4 * width : 4 * width + used]
     g1, b1, bq, bv, bo, g2, b2, bf2 = (small[:, i] for i in range(len(narrow)))

time: 431 us -> 517 us (1.20)
  waiting for transfers between devices: 320 us -> 391 us
  other arithmetic: 13.6 us -> 22.7 us
  starting transfers between devices: 0.46 us -> 5.75 us
    ppermute x0 -> x3, waiting for transfers between devices: none -> 207 us  [grow_blocks(): lax.ppermute(pieces, axis, [(i, i ^ stride) for i in range(size)])]
    all_gather x1, waiting for transfers between devices: 54.1 us -> 0.01 us  [body(): attn_all = lax.all_gather(packed, 'shard', axis=0, tiled=True)]
    all_gather x1, waiting for transfers between devices: 45.7 us -> 0.01 us  [body(): fc2_all = lax.all_gather(fc2_weight, 'shard', axis=0, tiled=True)]
    all_gather x1 -> x0, waiting for transfers between devices: 36.8 us -> none  [body(): fc1_all = lax.all_gather(fc1_weight, 'shard', axis=0, tiled=True)]
    ppermute x0 -> x3, starting transfers between devices: none -> 5.32 us  [grow_blocks(): lax.ppermute(pieces, axis, [(i, i ^ stride) for i in range(size)])]
  transfers between devices with their start and end apart: 7 -> 9, of which waited for: 7 -> 7; matrix products, arithmetic and copies ran while one was open for 16% -> 15% of each run, Pallas kernels for 0% -> 0%
where the time goes in v1:
time: 517 us; the launch traced here: 516 us
  waiting for transfers between devices  391 us (76%)
  matrix products  52.5 us (10%)
  local copies, waits for them, and re-layouts  29.1 us (6%)
  other arithmetic  22.7 us (4%)
  between operations  14.6 us (3%)
  starting transfers between devices  5.75 us (1%)
    ppermute x3, waiting for transfers between devices, grow_blocks(): lax.ppermute(pieces, axis, [(i, i ^ stride) for i in range(size)])  207 us
    reduce_scatter x3, waiting for transfers between devices, owned(): lax.psum_scatter(grad.astype(bf16), 'shard', scatter_dimension=0, tiled=T...  124 us
    psum x1, waiting for transfers between devices, owned(): return lax.psum(part, 'replica').astype(f32)  60 us
    dot_general x18, matrix products, matmul(): return jnp.einsum(spec, left, right, preferred_element_type=jnp.float32)  52.5 us
  transfers between devices with their start and end apart: 9, of which 7 were waited for; matrix products, arithmetic and copies ran while one was open for 15% of the time, Pallas kernels for 0%

profile of v1, /device:TPU:0, one launch (start us, length us, event | category | flops | bytes accessed | tf_op | source)
XLA Modules:
  0.0 515.8 jit_solution(26501159931037581)
XLA Ops:
  9.1 0.9 constant_dynamic-update-slice_fusion.3
  10.0 0.9 constant_dynamic-update-slice_fusion.2
  10.9 0.9 constant_dynamic-update-slice_fusion.1
  11.8 0.9 constant_dynamic-update-slice_fusion
  14.3 1.8 collective-permute-done
  16.1 1.2 pad_maximum_fusion.2
  17.6 3.0 collective-permute-start.1
  20.7 65.8 %collective-permute-done.1 = bf16[2,96,3072]{2,1,0:T(8,128)(2,1)} collective-permute-done((bf16[2,96,3072]{2,1,0:T(8,128)(2,1)S(1)}, bf16[2,96,3072]{2,1,0:T(8,128)(2,1)}, u32[]{:S(2)}, u32[]{:S(2)}) %collective-permute-start.1) | collective-permute-done | bytes 1179680 | tf_op jit(solution)/shard_map/ppermute | solution.py:21
  86.5 1.5 pad_maximum_fusion.1
  88.7 1.8 collective-permute-start.2
  90.8 139.7 %collective-permute-done.2 = bf16[4,96,3072]{2,1,0:T(8,128)(2,1)} collective-permute-done((bf16[4,96,3072]{2,1,0:T(8,128)(2,1)S(1)}, bf16[4,96,3072]{2,1,0:T(8,128)(2,1)}, u32[]{:S(2)}, u32[]{:S(2)}) %collective-permute-start.2) | collective-permute-done | bytes 2359328 | tf_op jit(solution)/shard_map/ppermute | solution.py:21
  230.4 2.1 pad_maximum_fusion
  232.5 3.4 reverse_select_fusion
  235.9 1.0 slice_convert_fusion.1
  237.2 3.1 convert_reduce_fusion
  240.3 3.0 convolution_bitcast_fusion
  243.5 0.9 copy.96
  244.4 0.9 copy.97
  245.5 1.8 fusion.57
  248.5 1.9 fusion.58
  250.6 5.9 %multiply_convert_fusion.1 = (bf16[224,3072]{1,0:T(8,128)(2,1)}, f32[224,3072]{1,0:T(8,128)}) fusion(f32[3072]{0:T(1024)S(1)} %reshape.437, bf16[768,3072]{1,0:T(8,128)(2,1)} %bitcast.137, f32[1,224,768]{2,1,0:T(8,128)S(1)} %get-tuple-element.62, f32[768]{0:T(1024)S(1)} %get-tuple-element.18, f32[768]{0:T(1024)S(1)} %get-tuple-element.19, ...), kind=kOutput, calls=%fused_computation.22 | convolution fusion | flops 1061953536 | bytes 9555712 | tf_op jit(solution)/shard_map/cld,df->clf/dot_general | solution.py:33
  256.6 5.2 %fusion.59 = (bf16[3072]{0:T(1024)(128)(2,1)S(1)}, bf16[224,3072]{1,0:T(8,128)(2,1)S(1)}) fusion(f32[224,3072]{1,0:T(8,128)} %get-tuple-element.64, bf16[3072,768]{1,0:T(8,128)(2,1)} %all-gather.5.cloned.1.call-done, f32[1,224,768]{2,1,0:T(8,128)} %param.18), kind=kOutput, calls=%fused_computation.129 | convolution fusion | flops 1064702976 | bytes 9541632 | tf_op jit(solution)/shard_map/cld,fd->clf/dot_general | solution.py:33
  261.8 1.2 copy-done.14
  263.0 3.8 convolution_convert_fusion.2
  267.1 5.1 convolution_convert_fusion.1
  272.2 1.1 reshape.428
  273.3 4.6 fusion.21
  281.8 2.6 convolution_convert_fusion.6
  284.4 1.9 copy.99
  286.3 2.4 fusion.54
  288.7 1.1 stack.99
  289.8 1.9 multiply_reduce_fusion
  292.2 1.1 copy-done
  293.8 1.1 stack.98
  294.9 2.0 convolution_convert_fusion.4
  297.0 3.7 fusion.22
  303.4 2.3 concatenate.20
  306.2 2.6 convolution_convert_fusion
  308.9 2.6 fusion.1
  311.5 10.8 %reduce-scatter.6.cloned.1.call-done = bf16[96,3072]{1,0:T(8,128)(2,1)} async-done(((bf16[768,3072]{1,0:T(8,128)(2,1)}), bf16[96,3072]{1,0:T(8,128)(2,1)}) %reduce-scatter.6.cloned.1.call-update) | async-done | bytes 589840 | tf_op jit(solution)/shard_map/reduce_scatter | solution.py:220
  322.4 55.5 %reduce-scatter.8.cloned.1.call-done = bf16[384,768]{1,0:T(8,128)(2,1)} async-done(((bf16[3072,768]{1,0:T(8,128)(2,1)}), bf16[384,768]{1,0:T(8,128)(2,1)}) %reduce-scatter.8.cloned.1.call-update) | async-done | bytes 589840 | tf_op jit(solution)/shard_map/reduce_scatter | solution.py:220
  377.9 57.4 %reduce-scatter.4.cloned.1.call-done = bf16[96,3200]{1,0:T(8,128)(2,1)} async-done(((bf16[768,3200]{1,0:T(8,128)(2,1)}), bf16[96,3200]{1,0:T(8,128)(2,1)}) %reduce-scatter.4.cloned.1.call-update) | async-done | bytes 614416 | tf_op jit(solution)/shard_map/reduce_scatter | solution.py:220
  435.4 2.2 fusion.25
  437.6 4.4 fusion.13
  442.0 60.0 %all-reduce.5.cloned.1.call-done = (bf16[96,3200]{1,0:T(8,128)(2,1)}, bf16[96,3072]{1,0:T(8,128)(2,1)}, bf16[384,768]{1,0:T(8,128)(2,1)}) async-done(((bf16[96,3200]{1,0:T(8,128)(2,1)}, bf16[96,3072]{1,0:T(8,128)(2,1)}, bf16[384,768]{1,0:T(8,128)(2,1)}), (bf16[96,3200]{1,0:T(8,128)(2,1)}, bf16[96,3072]{1,0:T(8,128)(2,1)}, bf16[384,768]{1,0:T(8,128)(2,1)})) %all-reduce.5.cloned.1.call-update) | async-done | bytes 1794064 | tf_op jit(solution)/shard_map/psum | solution.py:221
  502.9 2.2 fusion.56
  505.9 1.1 convert_element_type.259
  507.0 1.1 convert_element_type.261
  (107 shorter events, 17.6 us)
Async XLA Ops:
  7.2 228.7 %all-gather.3.cloned.1.call-start = ((), (), s32[]{:S(2)}) async-start(), calls=%async_computation.3 | async-start | bytes 5529600 | tf_op jit(solution)/shard_map/all_gather | solution.py:206
  12.8 0.8 copy-start.15
  13.6 242.9 %all-gather.5.cloned.1.call-start = ((), (), s32[]{:S(2)}) async-start(), calls=%async_computation.4 | async-start | bytes 5308416 | tf_op jit(solution)/shard_map/all_gather | solution.py:208
  13.7 2.4 collective-permute-start
  17.6 68.9 %collective-permute-start.1 = (bf16[2,96,3072]{2,1,0:T(8,128)(2,1)S(1)}, bf16[2,96,3072]{2,1,0:T(8,128)(2,1)}, u32[]{:S(2)}, u32[]{:S(2)}) collective-permute-start(bf16[2,96,3072]{2,1,0:T(8,128)(2,1)S(1)} %get-tuple-element.49), channel_id=1, source_target_pairs={{0,2},{1,3},{2,0},{3,1},{4,6},{5,7},{6,4},{7,5},{8,10},{9,11},{10,... | collective-permute-start | bytes 3538952 | tf_op jit(solution)/shard_map/ppermute | solution.py:21
  20.7 301.7 %reduce-scatter.6.cloned.1.call-start = ((), (), s32[]{:S(2)}) async-start(), calls=%async_computation.6 | async-start | bytes 5308416 | tf_op jit(solution)/shard_map/reduce_scatter | solution.py:220
  88.1 2.4 copy-start.1
  88.7 141.8 %collective-permute-start.2 = (bf16[4,96,3072]{2,1,0:T(8,128)(2,1)S(1)}, bf16[4,96,3072]{2,1,0:T(8,128)(2,1)}, u32[]{:S(2)}, u32[]{:S(2)}) collective-permute-start(bf16[4,96,3072]{2,1,0:T(8,128)(2,1)S(1)} %bitcast.135), channel_id=1, source_target_pairs={{0,4},{1,5},{2,6},{3,7},{4,0},{5,1},{6,2},{7,3},{8,12},{9,13},{10,... | collective-permute-start | bytes 7077896 | tf_op jit(solution)/shard_map/ppermute | solution.py:21
  245.5 2.3 copy-start.7
  247.4 1.1 copy-start.2
  248.4 2.0 copy-start.9
  261.8 1.2 copy-start.14
  266.8 111.1 %reduce-scatter.8.cloned.1.call-start = ((), (), s32[]{:S(2)}) async-start(), calls=%async_computation.7 | async-start | bytes 5308416 | tf_op jit(solution)/shard_map/reduce_scatter | solution.py:220
  272.2 163.1 %reduce-scatter.4.cloned.1.call-start = ((), (), s32[]{:S(2)}) async-start(), calls=%async_computation.5 | async-start | bytes 5529600 | tf_op jit(solution)/shard_map/reduce_scatter | solution.py:220
  273.3 4.7 copy-start.13
  278.4 3.5 copy-start.4
  291.6 1.7 copy-start.8
  292.2 1.1 copy-start
  293.3 3.6 copy-start.3
  293.3 3.6 copy-start.24
  293.8 3.1 copy-start.25
  296.9 3.8 copy-start.26
  296.9 6.5 %copy-start.16 = (bf16[768,4]{1,0:T(8,128)(2,1)S(1)}, bf16[768,4]{1,0:T(8,128)(2,1)}, u32[]{:S(2)}) copy-start(bf16[768,4]{1,0:T(8,128)(2,1)} %reshape.428) | copy-start | bytes 18436
  296.9 6.4 %copy-start.17 = (bf16[768,1]{1,0:T(8,128)(2,1)S(1)}, bf16[768,1]{1,0:T(8,128)(2,1)}, u32[]{:S(2)}) copy-start(bf16[768,1]{1,0:T(8,128)(2,1)} %stack.100) | copy-start | bytes 4612
  297.0 6.4 %copy-start.18 = (bf16[768,1]{1,0:T(8,128)(2,1)S(1)}, bf16[768,1]{1,0:T(8,128)(2,1)}, u32[]{:S(2)}) copy-start(bf16[768,1]{1,0:T(8,128)(2,1)} %stack.102) | copy-start | bytes 4612
  297.0 6.4 %copy-start.19 = (bf16[768,1]{1,0:T(8,128)(2,1)S(1)}, bf16[768,1]{1,0:T(8,128)(2,1)}, u32[]{:S(2)}) copy-start(bf16[768,1]{1,0:T(8,128)(2,1)} %stack.101) | copy-start | bytes 4612
  297.0 6.4 %copy-start.20 = (bf16[768,1]{1,0:T(8,128)(2,1)S(1)}, bf16[768,1]{1,0:T(8,128)(2,1)}, u32[]{:S(2)}) copy-start(bf16[768,1]{1,0:T(8,128)(2,1)} %stack.103) | copy-start | bytes 4612
  300.7 0.8 copy-start.12
  300.7 5.0 copy-start.5
  300.7 5.0 copy-start.10
  306.2 2.6 copy-start.21
  311.5 126.1 %copy-start.11 = (bf16[224,3072]{1,0:T(8,128)(2,1)S(1)}, bf16[224,3072]{1,0:T(8,128)(2,1)}, u32[]{:S(2)}) copy-start(bf16[224,3072]{1,0:T(8,128)(2,1)} %get-tuple-element.63) | copy-start | bytes 4128772
  311.5 190.5 %all-reduce.5.cloned.1.call-start = ((), (), s32[]{:S(2)}) async-start(), calls=%async_computation.8 | async-start | bytes 3588096 | tf_op jit(solution)/shard_map/psum | solution.py:221
  502.0 3.1 copy-start.6
  502.0 3.9 copy-start.23
  502.9 4.1 copy-start.22
Sparse Core Ops, SparseCore 0:
  13.8 73.9 all-gather.2
  89.4 112.2 all-gather.4
  267.0 55.3 reduce-scatter.5
  324.5 53.3 reduce-scatter.7
  380.1 55.1 reduce-scatter.3
  438.7 63.2 all-reduce.4
